TPU v7x, 32 devices: a whole 2x2x4 slice. The times are simulated.
32 devices in a mesh: groups: 2 (over x), tensor: 16 (over z, y, core).
Axes of the slice: x: 2, y: 2, z: 4, core: 2. Of those that a mesh axis runs over, the one named last changes fastest.
Arguments:
- tokens: bfloat16 [64, 8192], P(('groups', 'tensor')), parts along dimension 0, may hold values from -6 to 6
- cotangent: bfloat16 [64, 8192], P(('groups', 'tensor')), parts along dimension 0, may hold values from -6 to 6
- up_blocks: bfloat16 [512, 128, 128], P('tensor'), may hold values from -0.1875 to 0.1875
- gate_blocks: bfloat16 [512, 128, 128], P('tensor'), may hold values from -0.1875 to 0.1875
- down_blocks: bfloat16 [512, 128, 128], P('tensor'), may hold values from -0.21875 to 0.21875
- up_layout: int32 [512], P('tensor'), may hold values from 0 to 191, as said below
- gate_layout: int32 [512], P('tensor'), may hold values from 0 to 191, as said below
- down_layout: int32 [512], P('tensor'), may hold values from 0 to 191, as said below
- live_counts: int32 [3, 16], P(None, 'tensor'), may hold values from 4 to 32, as said below
Outputs:
- output: bfloat16 [64, 8192], P(('groups', 'tensor')), parts along dimension 0
- grad_tokens: bfloat16 [64, 8192], P(('groups', 'tensor')), parts along dimension 0
- grad_up: bfloat16 [1024, 128, 128], P(('groups', 'tensor')), parts along dimension 0
- grad_gate: bfloat16 [1024, 128, 128], P(('groups', 'tensor')), parts along dimension 0
- grad_down: bfloat16 [1024, 128, 128], P(('groups', 'tensor')), parts along dimension 0
There are 2 independent parts, one for each index of `groups`. A program takes and returns all parts, laid end to end along the dimension named above; an argument that names none is the same for every part. Nothing has to cross between parts.
Inputs may be any that keep to these rules, and one draw needn't show every extreme that they name: `up_layout`: within the 32 slots of one owner the codes of one matrix are all different. `gate_layout`: within the 32 slots of one owner the codes of one matrix are all different. `down_layout`: within the 32 slots of one owner the codes of one matrix are all different. `live_counts`: in each of the three rows some owner has exactly 32 live slots; slots past an owner's count hold blocks that are not used.
All inputs are finite; a program needn't handle non-finite values.
Results may differ from a plain program's by a relative error of at most 0.0051.
Values may be sent and summed in bfloat16 or wider, within the bound.
A program may use at most 64 MiB of HBM per device.

v0:
```python
import jax
import jax.numpy as jnp
from jax import lax
from jax.sharding import PartitionSpec as P

HB_DEV = 3


def slot_tables(layout, count, major_size):
    slot_total = layout.shape[0]
    major = layout // HB_DEV
    minor = layout % HB_DEV
    live_mask = (jnp.arange(slot_total) < count).astype(jnp.float32)
    major_hot = (major[:, None] == jnp.arange(major_size)[None, :]).astype(jnp.float32)
    minor_hot = (minor[:, None] == jnp.arange(HB_DEV)[None, :]).astype(jnp.float32)
    return (major, minor, live_mask, major_hot, minor_hot)


def local(
    tokens,
    cotangent,
    up_blocks,
    gate_blocks,
    down_blocks,
    up_layout,
    gate_layout,
    down_layout,
    live_counts,
):
    highest = lax.Precision.HIGHEST
    f32 = jnp.float32
    x_full = lax.all_gather(tokens, "tensor", axis=0, tiled=True)
    dy_full = lax.all_gather(cotangent, "tensor", axis=0, tiled=True)
    row_total = x_full.shape[0]
    block_size = up_blocks.shape[1]
    width_blocks = x_full.shape[1] // block_size
    x_split = x_full.reshape(row_total, width_blocks, block_size)
    count_trio = live_counts[:, 0]
    up_major, up_minor, up_live, up_rowhot, up_hidhot = slot_tables(
        up_layout, count_trio[0], width_blocks
    )
    gate_major, gate_minor, gate_live, gate_rowhot, gate_hidhot = slot_tables(
        gate_layout, count_trio[1], width_blocks
    )
    down_major, down_minor, down_live, down_colhot, down_hidhot = slot_tables(
        down_layout, count_trio[2], width_blocks
    )
    w_up = up_blocks * up_live[:, None, None].astype(jnp.bfloat16)
    w_gate = gate_blocks * gate_live[:, None, None].astype(jnp.bfloat16)
    w_down = down_blocks * down_live[:, None, None].astype(jnp.bfloat16)
    x_up = jnp.take(x_split, up_major, axis=1)
    x_gate = jnp.take(x_split, gate_major, axis=1)
    up_terms = jnp.einsum("tsi,sij->tsj", x_up, w_up, preferred_element_type=f32)
    gate_terms = jnp.einsum("tsi,sij->tsj", x_gate, w_gate, preferred_element_type=f32)
    up_value = jnp.einsum("tsj,sh->thj", up_terms, up_hidhot, precision=highest)
    gate_value = jnp.einsum("tsj,sh->thj", gate_terms, gate_hidhot, precision=highest)
    sig = 1.0 / (1.0 + jnp.exp(-gate_value))
    act = gate_value * sig
    hidden = (act * up_value).astype(jnp.bfloat16)
    hid_down = jnp.take(hidden, down_minor, axis=1)
    out_terms = jnp.einsum("tsj,sjk->tsk", hid_down, w_down, preferred_element_type=f32)
    partial_out = jnp.einsum("tsk,sc->tck", out_terms, down_colhot, precision=highest).reshape(
        row_total, -1
    )
    out_share = lax.psum_scatter(partial_out, "tensor", scatter_dimension=0, tiled=True)
    dy_split = dy_full.reshape(row_total, width_blocks, block_size)
    dy_down = jnp.take(dy_split, down_major, axis=1)
    dh_terms = jnp.einsum("tsk,sjk->tsj", dy_down, w_down, preferred_element_type=f32)
    d_hidden = jnp.einsum("tsj,sh->thj", dh_terms, down_hidhot, precision=highest)
    d_up = (d_hidden * act).astype(jnp.bfloat16)
    d_gate = (d_hidden * up_value * sig * (1.0 + gate_value * (1.0 - sig))).astype(jnp.bfloat16)
    dup_slots = jnp.take(d_up, up_minor, axis=1)
    dgate_slots = jnp.take(d_gate, gate_minor, axis=1)
    dx_up = jnp.einsum("tsj,sij->tsi", dup_slots, w_up, preferred_element_type=f32)
    dx_gate = jnp.einsum("tsj,sij->tsi", dgate_slots, w_gate, preferred_element_type=f32)
    partial_dx = jnp.einsum("tsi,sr->tri", dx_up, up_rowhot, precision=highest)
    partial_dx = partial_dx + jnp.einsum("tsi,sr->tri", dx_gate, gate_rowhot, precision=highest)
    partial_dx = partial_dx.reshape(row_total, -1)
    dx_share = lax.psum_scatter(partial_dx, "tensor", scatter_dimension=0, tiled=True)
    grad_up = (
        jnp.einsum("tsi,tsj->sij", x_up, dup_slots, preferred_element_type=f32)
        * up_live[:, None, None]
    ).astype(jnp.bfloat16)
    grad_gate = (
        jnp.einsum("tsi,tsj->sij", x_gate, dgate_slots, preferred_element_type=f32)
        * gate_live[:, None, None]
    ).astype(jnp.bfloat16)
    grad_down = (
        jnp.einsum("tsj,tsk->sjk", hid_down, dy_down, preferred_element_type=f32)
        * down_live[:, None, None]
    ).astype(jnp.bfloat16)
    return (
        out_share.astype(jnp.bfloat16),
        dx_share.astype(jnp.bfloat16),
        grad_up,
        grad_gate,
        grad_down,
    )


def solution(mesh):
    placed = (
        P(("groups", "tensor"), None),
        P(("groups", "tensor"), None),
        P("tensor", None, None),
        P("tensor", None, None),
        P("tensor", None, None),
        P("tensor"),
        P("tensor"),
        P("tensor"),
        P(None, "tensor"),
    )
    return jax.shard_map(
        local,
        mesh=mesh,
        in_specs=placed,
        out_specs=(
            P(("groups", "tensor"), None),
            P(("groups", "tensor"), None),
            P(("groups", "tensor"), None, None),
            P(("groups", "tensor"), None, None),
            P(("groups", "tensor"), None, None),
        ),
        check_vma=False,
    )
```

profile of v0, /device:TPU:0, one launch (start us, length us, event | category | flops | bytes accessed | tf_op | source)
XLA Modules:
  0.0 150.8 jit_solution(14236068998945516922)
XLA Ops:
  0.6 0.7 compare_and_fusion.1
  1.3 24.8 %all-gather = bf16[16,2,8192]{2,1,0:T(2,128)(2,1)S(1)} all-gather(bf16[1,2,8192]{2,1,0:T(2,128)(2,1)} %bitcast.118), channel_id=1, replica_groups=mesh['groups'=2,'tensor'=16] {'tensor'}, dimensions={0}, use_global_device_ids=true | all-gather | bytes 557056 | tf_op jit(solution)/shard_map/all_gather | solution.py:32
  26.9 0.6 gather_fusion.1
  27.5 0.6 fusion.74
  28.1 0.6 fusion.73
  29.3 0.6 fusion.13
  29.9 0.6 gather_fusion
  30.5 0.6 fusion.72
  31.2 1.7 %convolution_bitcast_fusion.2 = f32[32,32,128]{2,0,1:T(8,128)S(1)} fusion(bf16[32,128,128]{2,1,0:T(8,128)(2,1)} %param.16, bf16[32]{0:T(256)(128)(2,1)S(1)} %fusion.72, bf16[32,32,128]{2,1,0:T(8,128)(2,1)S(1)} %gather_fusion, pred[32]{0:T(512)(128)(4,1)S(1)} %get-tuple-element.26), kind=kOutput, calls=%fused_computation.12 | convolution fusion | flops 35782656 | bytes 1835104 | tf_op jit(solution)/shard_map/tsi,sij->tsj/dot_general | solution.py:54
  32.9 0.6 fusion.15
  33.5 18.9 %all-gather.1 = bf16[16,2,8192]{2,1,0:T(2,128)(2,1)S(1)} all-gather(bf16[1,2,8192]{2,1,0:T(2,128)(2,1)S(1)} %bitcast.119), channel_id=1, replica_groups=mesh['groups'=2,'tensor'=16] {'tensor'}, dimensions={0}, use_global_device_ids=true | all-gather | bytes 557056 | tf_op jit(solution)/shard_map/all_gather | solution.py:33
  53.2 0.6 gather_fusion.3
  54.3 1.9 %convolution_bitcast_fusion.5 = f32[32,32,128]{2,0,1:T(8,128)S(1)} fusion(bf16[32,128,128]{2,1,0:T(8,128)(2,1)} %param.17, bf16[32]{0:T(256)(128)(2,1)S(1)} %fusion.71, bf16[32,32,128]{2,1,0:T(8,128)(2,1)S(1)} %gather_fusion.3, pred[32]{0:T(512)(128)(4,1)S(1)} %get-tuple-element.13), kind=kOutput, calls=%fused_computation.15 | convolution fusion | flops 34209792 | bytes 1835104 | tf_op jit(solution)/shard_map/tsk,sjk->tsj/dot_general | solution.py:68
  56.3 0.6 fusion.9
  57.0 0.6 gather_fusion.4
  57.6 0.7 convolution_bitcast_fusion.4
  58.3 0.9 fusion.7
  59.3 1.3 gather_fusion.5
  60.6 1.7 %convolution_bitcast_fusion.3 = f32[32,32,128]{2,0,1:T(8,128)S(1)} fusion(bf16[32,128,128]{2,1,0:T(8,128)(2,1)S(1)} %copy-done.1, bf16[32]{0:T(256)(128)(2,1)S(1)} %fusion.72, bf16[32,32,128]{2,1,0:T(8,128)(2,1)} %gather_fusion.5, pred[32]{0:T(512)(128)(4,1)S(1)} %get-tuple-element.9), kind=kOutput, calls=%fused_computation.13 | convolution fusion | flops 34209792 | bytes 1835104 | tf_op jit(solution)/shard_map/tsj,sij->tsi/dot_general | solution.py:75
  62.2 1.0 convolution_add_fusion
  63.2 0.6 copy.82
  63.9 0.6 gather_fusion.2
  65.0 0.9 fusion.11
  65.9 0.6 copy.83
  66.5 73.7 %all-reduce.4 = (bf16[32,8192]{1,0:T(8,128)(2,1)}, bf16[32,8192]{1,0:T(8,128)(2,1)}) all-reduce(f32[32,8192]{1,0:T(8,128)S(1)} %bitcast.115, f32[32,8192]{1,0:T(8,128)S(1)} %bitcast.114), channel_id=2, replica_groups=mesh['groups'=2,'tensor'=16] {'tensor'}, use_global_device_ids=true, to_apply=%region_0.3.clone | all-reduce | flops 524288 | bytes 3145728
  140.2 0.6 dynamic-slice
  141.4 1.7 %dynamic-slice_convert_fusion = (bf16[2,8192]{1,0:T(2,128)(2,1)}, bf16[2,8192]{1,0:T(2,128)(2,1)}) fusion(bf16[32,8192]{1,0:T(8,128)(2,1)} %get-tuple-element.8, u32[]{:T(128)S(6)} %multiply.1, bf16[32,8192]{1,0:T(8,128)(2,1)} %get-tuple-element.7), kind=kLoop, calls=%fused_computation.59 | loop fusion | bytes 131076 | tf_op jit(solution)/shard_map/convert_element_type | solution.py:94
  143.1 0.6 compare_convert_fusion.1
  143.8 2.6 %multiply_convert_fusion.1 = bf16[32,128,128]{2,1,0:T(8,128)(2,1)} fusion(f32[32]{0:T(128)S(1)} %compare_convert_fusion.1, bf16[32,32,128]{2,1,0:T(8,128)(2,1)S(1)} %gather_fusion, pred[32]{0:T(512)(128)(4,1)S(1)} %get-tuple-element.26, bf16[32,32,128]{2,1,0:T(8,128)(2,1)} %gather_fusion.5, pred[32]{0:T(512)(128)(4,1)S(1)} %get-tuple-element.9), kind=kOutput, calls=%fused_computation.7 | convolution fusion | flops 34865152 | bytes 1573056 | tf_op jit(solution)/shard_map/tsi,tsj->sij/dot_general | solution.py:85
  146.3 0.6 compare_convert_fusion
  147.0 1.6 %multiply_convert_fusion.2 = bf16[32,128,128]{2,1,0:T(8,128)(2,1)} fusion(f32[32]{0:T(128)S(1)} %compare_convert_fusion, bf16[32,32,128]{2,1,0:T(8,128)(2,1)S(1)} %gather_fusion.1, pred[32]{0:T(512)(128)(4,1)S(1)} %get-tuple-element.31, bf16[32,32,128]{2,1,0:T(8,128)(2,1)S(1)} %gather_fusion.4, pred[32]{0:T(512)(128)(4,1)S(1)} %get-tuple-element.11), kind=kOutput, calls=%fused_computation.8 | convolution fusion | flops 34865152 | bytes 1573056 | tf_op jit(solution)/shard_map/tsi,tsj->sij/dot_general | solution.py:81
  149.2 1.6 %multiply_convert_fusion = bf16[32,128,128]{2,1,0:T(8,128)(2,1)} fusion(f32[32]{0:T(128)S(1)} %compare_convert_fusion.2, bf16[32,32,128]{2,1,0:T(8,128)(2,1)S(1)} %gather_fusion.2, pred[32]{0:T(512)(128)(4,1)S(1)} %get-tuple-element.24, bf16[32,32,128]{2,1,0:T(8,128)(2,1)S(1)} %gather_fusion.3, pred[32]{0:T(512)(128)(4,1)S(1)} %get-tuple-element.13), kind=kOutput, calls=%fused_computation.6 | convolution fusion | flops 34865152 | bytes 1573056 | tf_op jit(solution)/shard_map/tsj,tsk->sjk/dot_general | solution.py:89
  (39 shorter events, 3.7 us)
Async XLA Ops:
  26.5 1.0 copy-start.4
  26.5 2.2 %copy-start = (bf16[32,128,128]{2,1,0:T(8,128)(2,1)S(1)}, bf16[32,128,128]{2,1,0:T(8,128)(2,1)}, u32[]{:S(2)}) copy-start(bf16[32,128,128]{2,1,0:T(8,128)(2,1)} %param.15) | copy-start | bytes 3145732
  28.8 1.1 copy-start.5
  31.2 2.3 %copy-start.6 = (s32[32]{0:T(128)S(1)}, s32[32]{0:T(128)}, u32[]{:S(2)}) copy-start(s32[32]{0:T(128)} %param.20) | copy-start | bytes 388
  31.2 2.4 %copy-start.3 = (bf16[2,8192]{1,0:T(2,128)(2,1)S(1)}, bf16[2,8192]{1,0:T(2,128)(2,1)}, u32[]{:S(2)}) copy-start(bf16[2,8192]{1,0:T(2,128)(2,1)} %param.14) | copy-start | bytes 98308
  58.3 2.3 %copy-start.1 = (bf16[32,128,128]{2,1,0:T(8,128)(2,1)S(1)}, bf16[32,128,128]{2,1,0:T(8,128)(2,1)}, u32[]{:S(2)}) copy-start(bf16[32,128,128]{2,1,0:T(8,128)(2,1)} %param.16) | copy-start | bytes 3145732
  63.2 1.3 copy-start.2
  66.5 73.7 %copy-start.7 = (u32[32]{0:T(128)S(1)}, u32[32]{0:T(128)}, u32[]{:S(2)}) copy-start(u32[32]{0:T(128)} %constant.59) | copy-start | bytes 388
where the time goes:
time: 151 us
  blocking collectives  117 us (77%)
  matrix products  17.4 us (12%)
  local copies, waits for them, and re-layouts  9.91 us (7%)
  other arithmetic  4.48 us (3%)
  between operations  1.65 us (1%)
    unnamed x1, blocking collectives  73.7 us
    all_gather x1, blocking collectives, local(): x_full = lax.all_gather(tokens, 'tensor', axis=0, tiled=True)  24.8 us
    all_gather x1, blocking collectives, local(): dy_full = lax.all_gather(cotangent, 'tensor', axis=0, tiled=True)  18.9 us

commit v1 on v0

--- a/solution.py
+++ b/solution.py
@@ -29,8 +29,11 @@
 ):
     highest = lax.Precision.HIGHEST
     f32 = jnp.float32
-    x_full = lax.all_gather(tokens, "tensor", axis=0, tiled=True)
-    dy_full = lax.all_gather(cotangent, "tensor", axis=0, tiled=True)
+    x_full, dy_full = jnp.split(
+        lax.all_gather(jnp.concatenate([tokens, cotangent], axis=1), "tensor", axis=0, tiled=True),
+        [tokens.shape[1]],
+        axis=1,
+    )
     row_total = x_full.shape[0]
     block_size = up_blocks.shape[1]
     width_blocks = x_full.shape[1] // block_size

time: 151 us -> 161 us (1.066)
  blocking collectives: 117 us -> 73.7 us
  waiting for transfers between devices: 0 us -> 33.4 us
  between operations: 1.65 us -> 15 us
  local copies, waits for them, and re-layouts: 9.91 us -> 13.4 us
  other arithmetic: 4.48 us -> 7.49 us
    all_gather x2 -> x0, blocking collectives: 43.7 us -> none  [the longest x1 24.8 us: local(): x_full = lax.all_gather(tokens, 'tensor', axis=0, tiled=True)]
    all_gather x0 -> x1, waiting for transfers between devices: none -> 33.3 us  [local(): lax.all_gather(jnp.concatenate([tokens, cotangent], axis=1), 'tensor', ax...]
    unnamed x19 -> x11, local copies, waits for them, and re-layouts: 1.85 us -> 4.43 us
  transfers between devices with their start and end apart: 0 -> 1, of which waited for: 0 -> 1; matrix products, arithmetic and copies ran while one was open for 0% -> 5% of each run, Pallas kernels for 0% -> 0%
where the time goes in v1:
time: 161 us; the launch traced here: 160 us
  blocking collectives  73.7 us (46%)
  waiting for transfers between devices  33.4 us (21%)
  matrix products  17.4 us (11%)
  between operations  15 us (9%)
  local copies, waits for them, and re-layouts  13.4 us (8%)
  other arithmetic  7.49 us (5%)
    unnamed x1, blocking collectives  73.7 us
    all_gather x1, waiting for transfers between devices, local(): lax.all_gather(jnp.concatenate([tokens, cotangent], axis=1), 'tensor', ax...  33.3 us
    unnamed x11, local copies, waits for them, and re-layouts  4.43 us
  transfers between devices with their start and end apart: 1, of which 1 were waited for; matrix products, arithmetic and copies ran while one was open for 5% of the time, Pallas kernels for 0%

profile of v1, /device:TPU:0, one launch (start us, length us, event | category | flops | bytes accessed | tf_op | source)
XLA Modules:
  0.0 160.3 jit_solution(4732375541338344880)
XLA Ops:
  7.2 1.5 maximum_bitcast_fusion
  8.7 1.4 fusion.74
  10.1 0.6 fusion.72
  10.7 0.7 compare_convert_fusion.1
  11.4 0.7 fusion.73
  12.0 0.7 compare_convert_fusion
  12.7 0.7 fusion.71
  13.4 0.7 compare_convert_fusion.2
  14.0 1.2 dynamic-slice
  15.9 0.7 compare_and_fusion.1
  16.6 0.7 compare_and_fusion
  17.3 0.7 compare_and_fusion.2
  18.1 33.3 %all-gather.3.cloned.1.call-done = bf16[16,2,16384]{2,1,0:T(2,128)(2,1)} async-done(((bf16[1,2,16384]{2,1,0:T(2,128)(2,1)}), bf16[16,2,16384]{2,1,0:T(2,128)(2,1)}) %all-gather.3.cloned.1.call-update) | async-done | bytes 1048592 | tf_op jit(solution)/shard_map/all_gather | solution.py:33
  51.4 1.5 reshape.130
  53.2 0.6 gather_fusion.1
  55.2 0.6 gather_fusion
  55.8 1.7 %convolution_bitcast_fusion.2 = f32[32,32,128]{2,0,1:T(8,128)S(1)} fusion(bf16[32,128,128]{2,1,0:T(8,128)(2,1)} %param.16, bf16[32]{0:T(256)(128)(2,1)S(1)} %fusion.72, bf16[32,32,128]{2,1,0:T(8,128)(2,1)S(1)} %gather_fusion, pred[32]{0:T(512)(128)(4,1)S(1)} %get-tuple-element.28), kind=kOutput, calls=%fused_computation.12 | convolution fusion | flops 35782656 | bytes 1835104 | tf_op jit(solution)/shard_map/tsi,sij->tsj/dot_general | solution.py:57
  58.7 1.9 %convolution_bitcast_fusion.5 = f32[32,32,128]{2,0,1:T(8,128)S(1)} fusion(bf16[32,128,128]{2,1,0:T(8,128)(2,1)} %param.17, bf16[32]{0:T(256)(128)(2,1)S(1)} %fusion.71, bf16[32,32,128]{2,1,0:T(8,128)(2,1)S(1)} %gather_fusion.3, pred[32]{0:T(512)(128)(4,1)S(1)} %get-tuple-element.13), kind=kOutput, calls=%fused_computation.15 | convolution fusion | flops 34209792 | bytes 1835104 | tf_op jit(solution)/shard_map/tsk,sjk->tsj/dot_general | solution.py:71
  61.9 0.7 convolution_bitcast_fusion.4
  62.6 0.9 fusion.7
  63.6 1.3 gather_fusion.5
  64.9 1.7 %convolution_bitcast_fusion.3 = f32[32,32,128]{2,0,1:T(8,128)S(1)} fusion(bf16[32,128,128]{2,1,0:T(8,128)(2,1)S(1)} %copy-done.1, bf16[32]{0:T(256)(128)(2,1)S(1)} %fusion.72, bf16[32,32,128]{2,1,0:T(8,128)(2,1)} %gather_fusion.5, pred[32]{0:T(512)(128)(4,1)S(1)} %get-tuple-element.9), kind=kOutput, calls=%fused_computation.13 | convolution fusion | flops 34209792 | bytes 1835104 | tf_op jit(solution)/shard_map/tsj,sij->tsi/dot_general | solution.py:78
  66.6 0.9 convolution_add_fusion
  67.5 0.6 copy.86
  69.2 0.9 fusion.11
  70.2 0.6 copy.87
  70.8 73.7 %all-reduce.4 = (bf16[32,8192]{1,0:T(8,128)(2,1)}, bf16[32,8192]{1,0:T(8,128)(2,1)}) all-reduce(f32[32,8192]{1,0:T(8,128)S(1)} %bitcast.123, f32[32,8192]{1,0:T(8,128)S(1)} %bitcast.122), channel_id=2, replica_groups=mesh['groups'=2,'tensor'=16] {'tensor'}, use_global_device_ids=true, to_apply=%region_0.3.clone | all-reduce | flops 524288 | bytes 3145728
  144.5 1.6 dynamic-slice_convert_fusion
  146.1 1.6 dynamic-slice_convert_fusion.1
  147.6 2.6 %multiply_convert_fusion.1 = bf16[32,128,128]{2,1,0:T(8,128)(2,1)} fusion(f32[32]{0:T(128)S(1)} %compare_convert_fusion.1, bf16[32,32,128]{2,1,0:T(8,128)(2,1)S(1)} %gather_fusion, pred[32]{0:T(512)(128)(4,1)S(1)} %get-tuple-element.28, bf16[32,32,128]{2,1,0:T(8,128)(2,1)} %gather_fusion.5, pred[32]{0:T(512)(128)(4,1)S(1)} %get-tuple-element.9), kind=kOutput, calls=%fused_computation.7 | convolution fusion | flops 34865152 | bytes 1573056 | tf_op jit(solution)/shard_map/tsi,tsj->sij/dot_general | solution.py:88
  150.2 1.6 %multiply_convert_fusion.2 = bf16[32,128,128]{2,1,0:T(8,128)(2,1)} fusion(f32[32]{0:T(128)S(1)} %compare_convert_fusion, bf16[32,32,128]{2,1,0:T(8,128)(2,1)S(1)} %gather_fusion.1, pred[32]{0:T(512)(128)(4,1)S(1)} %get-tuple-element.33, bf16[32,32,128]{2,1,0:T(8,128)(2,1)S(1)} %gather_fusion.4, pred[32]{0:T(512)(128)(4,1)S(1)} %get-tuple-element.11), kind=kOutput, calls=%fused_computation.8 | convolution fusion | flops 34865152 | bytes 1573056 | tf_op jit(solution)/shard_map/tsi,tsj->sij/dot_general | solution.py:84
  151.9 1.6 %multiply_convert_fusion = bf16[32,128,128]{2,1,0:T(8,128)(2,1)} fusion(f32[32]{0:T(128)S(1)} %compare_convert_fusion.2, bf16[32,32,128]{2,1,0:T(8,128)(2,1)S(1)} %gather_fusion.2, pred[32]{0:T(512)(128)(4,1)S(1)} %get-tuple-element.26, bf16[32,32,128]{2,1,0:T(8,128)(2,1)S(1)} %gather_fusion.3, pred[32]{0:T(512)(128)(4,1)S(1)} %get-tuple-element.13), kind=kOutput, calls=%fused_computation.6 | convolution fusion | flops 34865152 | bytes 1573056 | tf_op jit(solution)/shard_map/tsj,tsk->sjk/dot_general | solution.py:92
  (28 shorter events, 5.3 us)
Async XLA Ops:
  7.2 44.2 %all-gather.3.cloned.1.call-start = ((), (), s32[]{:S(2)}) async-start(), calls=%async_computation | async-start | bytes 1114112 | tf_op jit(solution)/shard_map/all_gather | solution.py:33
  53.0 1.2 copy-start
  62.6 2.2 %copy-start.1 = (bf16[32,128,128]{2,1,0:T(8,128)(2,1)S(1)}, bf16[32,128,128]{2,1,0:T(8,128)(2,1)}, u32[]{:S(2)}) copy-start(bf16[32,128,128]{2,1,0:T(8,128)(2,1)} %param.16) | copy-start | bytes 3145732
  67.5 1.2 copy-start.2
Sparse Core Ops, SparseCore 0:
  10.7 40.6 all-gather.2
